TPU v7x, 512 devices: a whole 4x8x8 slice. The times are simulated.
512 devices in a mesh: scen: 8 (over x, core), bus: 64 (over y, z).
Axes of the slice: x: 4, y: 8, z: 8, core: 2. Of those that a mesh axis runs over, the one named last changes fastest.
Arguments:
- injections: bfloat16 [1024, 16384], P(('scen', 'bus')), may hold values from -6 to 6
- tile_values: bfloat16 [4096, 128, 128], P('bus', 'scen'), may hold values from -0.109375 to 0.109375
- tile_line: int32 [4096], P('bus'), may hold values from 0 to 191, as said below
- tile_bus: int32 [4096], P('bus'), may hold values from 0 to 1
- flow_pred: bfloat16 [1024, 24576], P('scen', 'bus'), may hold values from -6 to 6
- line_limit: int32 [24576], P('bus'), may hold values from 50 to 199
Outputs:
- grad_injections: bfloat16 [1024, 16384], P(('scen', 'bus'))
- flows: float32 [1024, 24576], P('scen', 'bus')
Inputs may be any that keep to these rules, and one draw needn't show every extreme that they name: `tile_line`: tile t is held by bus index t // 64; line block b is owned by bus index b // 3. Of the 64 tiles of one bus index at most 2 have line blocks of one owner, and in every draw some owner gets exactly 2 tiles from every bus index. A pair of line block and bus block may occur in several tiles; their values add.
All inputs are finite; a program needn't handle non-finite values.
Results may differ from a plain program's by a relative error of at most 0.0039.
Values may be sent and summed in bfloat16 or wider, within the bound.
No kernel may reach another device: no remote copies, remote signals or barrier semaphores. Data moves between devices by JAX's collectives and lax.ppermute only.
A program may use at most 64 MiB of HBM per device.

v0:
```python
import jax
import jax.numpy as jnp
from jax import lax
from jax.sharding import PartitionSpec as P


def per_device(injections, tile_values, tile_line, tile_bus, flow_pred, line_limit):
    bus_count = lax.axis_size("bus")
    local_inj = lax.all_to_all(injections, "bus", split_axis=1, concat_axis=0, tiled=True)
    tile_full = lax.all_gather(tile_values, "scen", axis=1, tiled=True)
    tile_count = tile_full.shape[0]
    tile_size = tile_full.shape[1]
    row_count = local_inj.shape[0]
    blocks_here = local_inj.shape[1] // tile_size
    line_blocks = flow_pred.shape[1] // tile_size
    per_owner = tile_count // bus_count
    capacity = per_owner + max(1, tile_count // (2 * bus_count))
    slot_total = bus_count * capacity
    inj_blocks = local_inj.reshape(row_count, blocks_here, tile_size)
    per_tile_inj = jnp.take(inj_blocks, tile_bus, axis=1)
    partial_flows = jnp.einsum(
        "stb,tlb->tsl", per_tile_inj, tile_full, preferred_element_type=jnp.float32
    )
    owner_index = tile_line // line_blocks
    within_owner = tile_line % line_blocks
    owner_hits = (owner_index[:, None] == jnp.arange(bus_count, dtype=jnp.int32)[None, :]).astype(
        jnp.int32
    )
    rank_within = jnp.sum(jnp.cumsum(owner_hits, axis=0) * owner_hits, axis=1) - 1
    slot_index = owner_index * capacity + rank_within
    send_buffer = (
        jnp.zeros((slot_total, row_count, tile_size), jnp.float32).at[slot_index].set(partial_flows)
    )
    slot_label = jnp.full((slot_total,), -1, jnp.int32).at[slot_index].set(within_owner)
    received, received_label = (
        lax.all_to_all(send_buffer, "bus", split_axis=0, concat_axis=0, tiled=True),
        lax.all_to_all(slot_label, "bus", split_axis=0, concat_axis=0, tiled=True),
    )
    select_mask = (
        received_label[None, :] == jnp.arange(line_blocks, dtype=jnp.int32)[:, None]
    ).astype(jnp.float32)
    flow_blocks = jnp.einsum("ms,srl->rml", select_mask, received, precision=lax.Precision.HIGHEST)
    flows = flow_blocks.reshape(row_count, line_blocks * tile_size)
    line_cap = line_limit.astype(jnp.float32) * 0.01
    residual = flows - flow_pred.astype(jnp.float32)
    grad_flow = (
        residual
        + jax.nn.sigmoid(4.0 * (flows - line_cap))
        - jax.nn.sigmoid(4.0 * (-flows - line_cap))
    ).astype(jnp.bfloat16)
    gathered = lax.all_gather(grad_flow, "bus", axis=1, tiled=True)
    gathered_blocks = gathered.reshape(row_count, gathered.shape[1] // tile_size, tile_size)
    per_tile_grad = jnp.take(gathered_blocks, tile_line, axis=1)
    contrib = jnp.einsum(
        "stl,tlb->stb", per_tile_grad, tile_full, preferred_element_type=jnp.float32
    )
    bus_select = (tile_bus[:, None] == jnp.arange(blocks_here, dtype=jnp.int32)[None, :]).astype(
        jnp.float32
    )
    grad_blocks_bus = jnp.einsum(
        "stb,tk->skb", contrib, bus_select, precision=lax.Precision.HIGHEST
    )
    grad_local = grad_blocks_bus.reshape(row_count, blocks_here * tile_size).astype(jnp.bfloat16)
    grad_injections = lax.all_to_all(grad_local, "bus", split_axis=0, concat_axis=1, tiled=True)
    return (grad_injections, flows)


def solution(mesh):
    return jax.shard_map(
        per_device,
        mesh=mesh,
        in_specs=(
            P(("scen", "bus"), None),
            P("bus", "scen", None),
            P("bus"),
            P("bus"),
            P("scen", "bus"),
            P("bus"),
        ),
        out_specs=(P(("scen", "bus"), None), P("scen", "bus")),
        check_vma=False,
    )
```

profile of v0, /device:TPU:2, one launch (start us, length us, event | category | flops | bytes accessed | tf_op | source)
XLA Modules:
  0.0 535.0 jit_solution(14193557377811817124)
XLA Ops:
  7.2 0.7 all-gather.3.cloned.1.call-update
  7.9 16.6 %all-to-all-start = ((bf16[2,64,256]{2,0,1:T(2,128)(2,1)}), bf16[2,64,256]{2,0,1:T(2,128)(2,1)S(1)}, u32[]{:S(2)}, u32[]{:S(2)}) async-start(bf16[2,64,256]{2,0,1:T(2,128)(2,1)} %bitcast.34), calls=%async_computation | async-start | bytes 131072 | tf_op jit(solution)/shard_map/all_to_all | solution.py:9
  26.9 0.8 scatter_custom_fusion.1
  27.6 0.8 all_to_all.37
  28.4 8.4 %all-to-all-done = bf16[2,64,256]{2,0,1:T(2,128)(2,1)S(1)} async-done(((bf16[2,64,256]{2,0,1:T(2,128)(2,1)}), bf16[2,64,256]{2,0,1:T(2,128)(2,1)S(1)}, u32[]{:S(2)}, u32[]{:S(2)}) %all-to-all-start) | async-done | bytes 65568 | tf_op jit(solution)/shard_map/all_to_all | solution.py:9
  36.8 4.6 all-to-all-start.2
  41.4 1.0 gather_fusion
  42.4 4.4 all-gather.3.cloned.1.call-done
  46.9 5.2 fusion.5
  52.0 4.3 broadcast_in_dim.41
  56.3 12.0 %scatter_fusion = f32[128,128,128]{2,1,0:T(8,128)} fusion(f32[128,128,128]{2,1,0:T(8,128)} %broadcast_in_dim.41, s32[64]{0:T(128)S(1)} %compare_select_fusion.1, f32[64,128,128]{2,1,0:T(8,128)} %fusion.5), kind=kCustom, calls=%fused_computation.2 | custom fusion | bytes 12583168 | tf_op jit(solution)/shard_map/scatter | solution.py:32
  68.4 13.8 %all-to-all-start.1 = ((f32[128,128,128]{2,1,0:T(8,128)}), f32[128,128,128]{2,1,0:T(8,128)}, u32[]{:S(2)}, u32[]{:S(2)}) async-start(f32[128,128,128]{2,1,0:T(8,128)} %scatter_fusion), calls=%async_computation.1 | async-start | bytes 16777216 | tf_op jit(solution)/shard_map/all_to_all | solution.py:36
  83.0 0.7 reduce.3
  83.9 234.9 %all-to-all-done.1 = f32[128,128,128]{2,1,0:T(8,128)} async-done(((f32[128,128,128]{2,1,0:T(8,128)}), f32[128,128,128]{2,1,0:T(8,128)}, u32[]{:S(2)}, u32[]{:S(2)}) %all-to-all-start.1) | async-done | bytes 8388640 | tf_op jit(solution)/shard_map/all_to_all | solution.py:36
  318.8 10.4 %fusion.11 = f32[128,3,128]{2,1,0:T(4,128)S(1)} fusion(f32[128,128,128]{2,1,0:T(8,128)} %all-to-all-done.1, s32[128]{0:T(128)S(1)} %eq.49), kind=kOutput, calls=%fused_computation.16 | convolution fusion | flops 75497856 | bytes 8585728 | tf_op jit(solution)/shard_map/ms,srl->rml/dot_general | solution.py:42
  329.4 0.8 subtract_convert_fusion
  330.3 157.1 %all-gather.5.cloned.1.call-done = bf16[128,24576]{0,1:T(8,128)(2,1)} async-done(((bf16[128,384]{0,1:T(8,128)(2,1)}), bf16[128,24576]{0,1:T(8,128)(2,1)}) %all-gather.5.cloned.1.call-update) | async-done | bytes 6291472 | tf_op jit(solution)/shard_map/all_gather | solution.py:51
  487.4 8.7 %copy.31 = bf16[128,192,128]{2,0,1:T(8,128)(2,1)} copy(bf16[128,192,128]{0,2,1:T(8,128)(2,1)} %bitcast.30) | data formatting | bytes 12582912 | tf_op jit(solution)/shard_map/reshape | solution.py:52
  496.0 3.7 gather_fusion.1
  499.8 2.4 convolution_bitcast_fusion
  502.1 3.8 fusion.17
  506.6 8.6 %all-to-all-start.3 = ((bf16[64,2,256]{2,1,0:T(2,128)(2,1)}), bf16[64,2,256]{2,1,0:T(2,128)(2,1)S(1)}, u32[]{:S(2)}, u32[]{:S(2)}) async-start(bf16[64,2,256]{2,1,0:T(2,128)(2,1)} %convert_element_type.30), calls=%async_computation.3 | async-start | bytes 131072 | tf_op jit(solution)/shard_map/all_to_all | solution.py:64
  515.2 0.8 copy.34
  516.0 11.5 %all-to-all-done.3 = bf16[64,2,256]{2,1,0:T(2,128)(2,1)S(1)} async-done(((bf16[64,2,256]{2,1,0:T(2,128)(2,1)}), bf16[64,2,256]{2,1,0:T(2,128)(2,1)S(1)}, u32[]{:S(2)}, u32[]{:S(2)}) %all-to-all-start.3) | async-done | bytes 65568 | tf_op jit(solution)/shard_map/all_to_all | solution.py:64
  (31 shorter events, 4.9 us)
Async XLA Ops:
  7.2 39.7 %all-gather.3.cloned.1.call-start = ((), (), s32[]{:S(2)}) async-start(), calls=%async_computation.4 | async-start | bytes 2359296 | tf_op jit(solution)/shard_map/all_gather | solution.py:10
  7.9 28.9 %all-to-all-start = ((bf16[2,64,256]{2,0,1:T(2,128)(2,1)}), bf16[2,64,256]{2,0,1:T(2,128)(2,1)S(1)}, u32[]{:S(2)}, u32[]{:S(2)}) async-start(bf16[2,64,256]{2,0,1:T(2,128)(2,1)} %bitcast.34), calls=%async_computation | async-start | bytes 131072 | tf_op jit(solution)/shard_map/all_to_all | solution.py:9
  36.8 31.6 %all-to-all-start.2 = ((s32[64,2,1]{1,2,0:T(1,128)}), s32[64,2,1]{1,2,0:T(1,128)S(1)}, u32[]{:S(2)}, u32[]{:S(2)}) async-start(s32[64,2,1]{1,2,0:T(1,128)} %bitcast.4), calls=%async_computation.2 | async-start | bytes 65536 | tf_op jit(solution)/shard_map/all_to_all | solution.py:37
  68.3 14.0 %copy-start = (bf16[128,384]{1,0:T(8,128)(2,1)S(1)}, bf16[128,384]{1,0:T(8,128)(2,1)}, u32[]{:S(2)}) copy-start(bf16[128,384]{1,0:T(8,128)(2,1)} %param.10) | copy-start | bytes 294916
  68.3 14.1 %copy-start.1 = (s32[384]{0:T(512)S(1)}, s32[384]{0:T(512)}, u32[]{:S(2)}) copy-start(s32[384]{0:T(512)} %param.11) | copy-start | bytes 4612
  68.4 250.5 %all-to-all-start.1 = ((f32[128,128,128]{2,1,0:T(8,128)}), f32[128,128,128]{2,1,0:T(8,128)}, u32[]{:S(2)}, u32[]{:S(2)}) async-start(f32[128,128,128]{2,1,0:T(8,128)} %scatter_fusion), calls=%async_computation.1 | async-start | bytes 16777216 | tf_op jit(solution)/shard_map/all_to_all | solution.py:36
  82.1 405.2 %all-gather.5.cloned.1.call-start = ((), (), s32[]{:S(2)}) async-start(), calls=%async_computation.5 | async-start | bytes 6389760 | tf_op jit(solution)/shard_map/all_gather | solution.py:51
  83.9 246.4 %copy-start.3 = (s32[64]{0:T(128)S(1)}, s32[64]{0:T(128)}, u32[]{:S(2)}) copy-start(s32[64]{0:T(128)} %param.8) | copy-start | bytes 772
  499.8 2.4 copy-start.2
  506.6 20.9 %all-to-all-start.3 = ((bf16[64,2,256]{2,1,0:T(2,128)(2,1)}), bf16[64,2,256]{2,1,0:T(2,128)(2,1)S(1)}, u32[]{:S(2)}, u32[]{:S(2)}) async-start(bf16[64,2,256]{2,1,0:T(2,128)(2,1)} %convert_element_type.30), calls=%async_computation.3 | async-start | bytes 131072 | tf_op jit(solution)/shard_map/all_to_all | solution.py:64
Sparse Core Ops, SparseCore 0:
  10.1 36.6 all-gather.2
  330.4 156.9 all-gather.4
where the time goes:
time: 536 us; the launch traced here: 535 us
  waiting for transfers between devices  417 us (78%)
  starting transfers between devices  43.8 us (8%)
  local copies, waits for them, and re-layouts  34.3 us (6%)
  matrix products  21.8 us (4%)
  between operations  14.2 us (3%)
    all_to_all x1, waiting for transfers between devices, per_device(): lax.all_to_all(send_buffer, 'bus', split_axis=0, concat_axis=0, tiled=True)  235 us
    all_gather x1, waiting for transfers between devices, per_device(): gathered = lax.all_gather(grad_flow, 'bus', axis=1, tiled=True)  157 us
    all_to_all x1, starting transfers between devices, per_device(): lax.all_to_all(injections, 'bus', split_axis=1, concat_axis=0, tiled=True)  16.6 us
    all_to_all x1, starting transfers between devices, per_device(): lax.all_to_all(send_buffer, 'bus', split_axis=0, concat_axis=0, tiled=True)  13.8 us
    scatter x1, local copies, waits for them, and re-layouts, per_device(): jnp.zeros((slot_total, row_count, tile_size), jnp.float32).at[slot_index]  12 us
    all_to_all x1, waiting for transfers between devices, per_device(): lax.all_to_all(grad_local, 'bus', split_axis=0, concat_axis=1, tiled=True)  11.5 us
  transfers between devices with their start and end apart: 6, of which 5 were waited for; matrix products, arithmetic and copies ran while one was open for 5% of the time, Pallas kernels for 0%

commit v1 on v0

--- a/solution.py
+++ b/solution.py
@@ -48,7 +48,11 @@
         + jax.nn.sigmoid(4.0 * (flows - line_cap))
         - jax.nn.sigmoid(4.0 * (-flows - line_cap))
     ).astype(jnp.bfloat16)
-    gathered = lax.all_gather(grad_flow, "bus", axis=1, tiled=True)
+    size = lax.axis_size("bus")
+    repeats = [size if d == 1 else 1 for d in range(grad_flow.ndim)]
+    gathered = lax.all_to_all(
+        jnp.tile(grad_flow, repeats), "bus", split_axis=1, concat_axis=1, tiled=True
+    )
     gathered_blocks = gathered.reshape(row_count, gathered.shape[1] // tile_size, tile_size)
     per_tile_grad = jnp.take(gathered_blocks, tile_line, axis=1)
     contrib = jnp.einsum(

time: 536 us -> 658 us (1.23)
  the two profiles are of different devices: /device:TPU:2 before, /device:TPU:8 now
where the time goes in v1:
time: 658 us; the launch traced here: 657 us
  waiting for transfers between devices  462 us (70%)
  starting transfers between devices  117 us (18%)
  local copies, waits for them, and re-layouts  38.3 us (6%)
  matrix products  21.7 us (3%)
  between operations  14.2 us (2%)
    all_to_all x1, waiting for transfers between devices, per_device(): lax.all_to_all(send_buffer, 'bus', split_axis=0, concat_axis=0, tiled=True)  250 us
    all_to_all x1, waiting for transfers between devices, per_device(): lax.all_to_all(jnp.tile(grad_flow, repeats), 'bus', split_axis=1, concat_...  188 us
    all_to_all x1, starting transfers between devices, per_device(): lax.all_to_all(jnp.tile(grad_flow, repeats), 'bus', split_axis=1, concat_...  49.9 us
    all_to_all x1, starting transfers between devices, per_device(): lax.all_to_all(grad_local, 'bus', split_axis=0, concat_axis=1, tiled=True)  31.7 us
    all_to_all x1, starting transfers between devices, per_device(): lax.all_to_all(injections, 'bus', split_axis=1, concat_axis=0, tiled=True)  16.6 us
    all_to_all x1, starting transfers between devices, per_device(): lax.all_to_all(send_buffer, 'bus', split_axis=0, concat_axis=0, tiled=True)  13.8 us
  transfers between devices with their start and end apart: 6, of which 5 were waited for; matrix products, arithmetic and copies ran while one was open for 4% of the time, Pallas kernels for 0%

profile of v1, /device:TPU:8, one launch (start us, length us, event | category | flops | bytes accessed | tf_op | source)
XLA Modules:
  0.0 656.7 jit_solution(9815568015619625779)
XLA Ops:
  7.9 16.6 %all-to-all-start = ((bf16[2,64,256]{2,0,1:T(2,128)(2,1)}), bf16[2,64,256]{2,0,1:T(2,128)(2,1)S(1)}, u32[]{:S(2)}, u32[]{:S(2)}) async-start(bf16[2,64,256]{2,0,1:T(2,128)(2,1)} %bitcast.33), calls=%async_computation | async-start | bytes 131072 | tf_op jit(solution)/shard_map/all_to_all | solution.py:9
  26.9 0.8 scatter_custom_fusion.1
  27.6 0.8 all_to_all.41
  28.4 7.5 %all-to-all-done = bf16[2,64,256]{2,0,1:T(2,128)(2,1)S(1)} async-done(((bf16[2,64,256]{2,0,1:T(2,128)(2,1)}), bf16[2,64,256]{2,0,1:T(2,128)(2,1)S(1)}, u32[]{:S(2)}, u32[]{:S(2)}) %all-to-all-start) | async-done | bytes 65568 | tf_op jit(solution)/shard_map/all_to_all | solution.py:9
  35.9 5.4 all-to-all-start.2
  41.4 1.0 gather_fusion
  42.3 4.9 all-gather.2.cloned.1.call-done
  47.2 5.2 fusion.5
  52.4 4.3 broadcast_in_dim.41
  56.7 11.9 %scatter_fusion = f32[128,128,128]{2,1,0:T(8,128)} fusion(f32[128,128,128]{2,1,0:T(8,128)} %broadcast_in_dim.41, s32[64]{0:T(128)S(1)} %compare_select_fusion.1, f32[64,128,128]{2,1,0:T(8,128)} %fusion.5), kind=kCustom, calls=%fused_computation.2 | custom fusion | bytes 12583168 | tf_op jit(solution)/shard_map/scatter | solution.py:32
  68.6 13.8 %all-to-all-start.1 = ((f32[128,128,128]{2,1,0:T(8,128)}), f32[128,128,128]{2,1,0:T(8,128)}, u32[]{:S(2)}, u32[]{:S(2)}) async-start(f32[128,128,128]{2,1,0:T(8,128)} %scatter_fusion), calls=%async_computation.1 | async-start | bytes 16777216 | tf_op jit(solution)/shard_map/all_to_all | solution.py:36
  83.1 0.7 reduce.3
  84.0 250.0 %all-to-all-done.1 = f32[128,128,128]{2,1,0:T(8,128)} async-done(((f32[128,128,128]{2,1,0:T(8,128)}), f32[128,128,128]{2,1,0:T(8,128)}, u32[]{:S(2)}, u32[]{:S(2)}) %all-to-all-start.1) | async-done | bytes 8388640 | tf_op jit(solution)/shard_map/all_to_all | solution.py:36
  334.0 10.4 %fusion.11 = f32[128,3,128]{2,1,0:T(4,128)S(1)} fusion(f32[128,128,128]{2,1,0:T(8,128)} %all-to-all-done.1, s32[128]{0:T(128)S(1)} %eq.49), kind=kOutput, calls=%fused_computation.16 | convolution fusion | flops 75497856 | bytes 8585728 | tf_op jit(solution)/shard_map/ms,srl->rml/dot_general | solution.py:42
  344.8 4.2 tile.2
  349.0 49.9 %all-to-all-start.3 = ((bf16[128,64,384]{0,2,1:T(8,128)(2,1)}), bf16[128,64,384]{0,2,1:T(8,128)(2,1)}, u32[]{:S(2)}, u32[]{:S(2)}) async-start(bf16[128,64,384]{0,2,1:T(8,128)(2,1)} %tile.2), calls=%async_computation.3 | async-start | bytes 12582912 | tf_op jit(solution)/shard_map/all_to_all | solution.py:53
  398.9 188.0 %all-to-all-done.3 = bf16[128,64,384]{0,2,1:T(8,128)(2,1)} async-done(((bf16[128,64,384]{0,2,1:T(8,128)(2,1)}), bf16[128,64,384]{0,2,1:T(8,128)(2,1)}, u32[]{:S(2)}, u32[]{:S(2)}) %all-to-all-start.3) | async-done | bytes 6291488 | tf_op jit(solution)/shard_map/all_to_all | solution.py:53
  586.8 8.6 %copy.32 = bf16[128,192,128]{2,0,1:T(8,128)(2,1)} copy(bf16[128,192,128]{0,2,1:T(8,128)(2,1)} %bitcast.8) | data formatting | bytes 12582912 | tf_op jit(solution)/shard_map/reshape | solution.py:56
  595.4 3.7 gather_fusion.1
  599.2 2.4 convolution_bitcast_fusion
  601.6 3.8 fusion.17
  606.1 31.7 %all-to-all-start.4 = ((bf16[64,2,256]{2,1,0:T(2,128)(2,1)}), bf16[64,2,256]{2,1,0:T(2,128)(2,1)S(1)}, u32[]{:S(2)}, u32[]{:S(2)}) async-start(bf16[64,2,256]{2,1,0:T(2,128)(2,1)} %convert_element_type.30), calls=%async_computation.4 | async-start | bytes 131072 | tf_op jit(solution)/shard_map/all_to_all | solution.py:68
  637.8 0.8 copy.35
  638.6 10.6 %all-to-all-done.4 = bf16[64,2,256]{2,1,0:T(2,128)(2,1)S(1)} async-done(((bf16[64,2,256]{2,1,0:T(2,128)(2,1)}), bf16[64,2,256]{2,1,0:T(2,128)(2,1)S(1)}, u32[]{:S(2)}, u32[]{:S(2)}) %all-to-all-start.4) | async-done | bytes 65568 | tf_op jit(solution)/shard_map/all_to_all | solution.py:68
  (31 shorter events, 5.6 us)
Async XLA Ops:
  7.2 40.1 %all-gather.2.cloned.1.call-start = ((), (), s32[]{:S(2)}) async-start(), calls=%async_computation.5 | async-start | bytes 2359296 | tf_op jit(solution)/shard_map/all_gather | solution.py:10
  7.9 28.0 %all-to-all-start = ((bf16[2,64,256]{2,0,1:T(2,128)(2,1)}), bf16[2,64,256]{2,0,1:T(2,128)(2,1)S(1)}, u32[]{:S(2)}, u32[]{:S(2)}) async-start(bf16[2,64,256]{2,0,1:T(2,128)(2,1)} %bitcast.33), calls=%async_computation | async-start | bytes 131072 | tf_op jit(solution)/shard_map/all_to_all | solution.py:9
  35.9 32.7 %all-to-all-start.2 = ((s32[64,2,1]{1,2,0:T(1,128)}), s32[64,2,1]{1,2,0:T(1,128)S(1)}, u32[]{:S(2)}, u32[]{:S(2)}) async-start(s32[64,2,1]{1,2,0:T(1,128)} %bitcast.4), calls=%async_computation.2 | async-start | bytes 65536 | tf_op jit(solution)/shard_map/all_to_all | solution.py:37
  68.6 13.8 %copy-start = (bf16[128,384]{1,0:T(8,128)(2,1)S(1)}, bf16[128,384]{1,0:T(8,128)(2,1)}, u32[]{:S(2)}) copy-start(bf16[128,384]{1,0:T(8,128)(2,1)} %param.10) | copy-start | bytes 294916
  68.6 14.0 %copy-start.1 = (s32[384]{0:T(512)S(1)}, s32[384]{0:T(512)}, u32[]{:S(2)}) copy-start(s32[384]{0:T(512)} %param.11) | copy-start | bytes 4612
  68.6 265.4 %all-to-all-start.1 = ((f32[128,128,128]{2,1,0:T(8,128)}), f32[128,128,128]{2,1,0:T(8,128)}, u32[]{:S(2)}, u32[]{:S(2)}) async-start(f32[128,128,128]{2,1,0:T(8,128)} %scatter_fusion), calls=%async_computation.1 | async-start | bytes 16777216 | tf_op jit(solution)/shard_map/all_to_all | solution.py:36
  349.0 49.9 %copy-start.3 = (s32[64]{0:T(128)S(1)}, s32[64]{0:T(128)}, u32[]{:S(2)}) copy-start(s32[64]{0:T(128)} %param.8) | copy-start | bytes 772
  349.0 237.9 %all-to-all-start.3 = ((bf16[128,64,384]{0,2,1:T(8,128)(2,1)}), bf16[128,64,384]{0,2,1:T(8,128)(2,1)}, u32[]{:S(2)}, u32[]{:S(2)}) async-start(bf16[128,64,384]{0,2,1:T(8,128)(2,1)} %tile.2), calls=%async_computation.3 | async-start | bytes 12582912 | tf_op jit(solution)/shard_map/all_to_all | solution.py:53
  599.2 2.4 copy-start.2
  606.1 43.1 %all-to-all-start.4 = ((bf16[64,2,256]{2,1,0:T(2,128)(2,1)}), bf16[64,2,256]{2,1,0:T(2,128)(2,1)S(1)}, u32[]{:S(2)}, u32[]{:S(2)}) async-start(bf16[64,2,256]{2,1,0:T(2,128)(2,1)} %convert_element_type.30), calls=%async_computation.4 | async-start | bytes 131072 | tf_op jit(solution)/shard_map/all_to_all | solution.py:68
Sparse Core Ops, SparseCore 0:
  10.1 37.0 all-gather.1
